TPU v7x, 512 devices: a whole 4x4x16 slice. The times are simulated.
512 devices in a mesh: loop: 32 (over x, z_lo, core), grp: 16 (over z_hi, y).
Axes of the slice: x: 4, y: 4, z: 16 (z_hi: 4, z_lo: 4; z = z_hi * 4 + z_lo), core: 2. Of those that a mesh axis runs over, the one named last changes fastest.
Arguments:
- adjacency_tiles: bfloat16 [65536, 128, 128], P(('loop', 'grp')), may hold values from -0.046875 to 0.046875
- row_block: int32 [65536], P(('loop', 'grp')), may hold values from 0 to 31
- column_block: int32 [65536], P(('loop', 'grp')), may hold values from 0 to 15
- features: bfloat16 [65536, 256], P(('loop', 'grp')), may hold values from -6 to 6
- weight: bfloat16 [256, 256], replicated, may hold values from -0.375 to 0.375
- out_bias: float32 [256], replicated, may hold values from -3 to 3
Outputs:
- result: bfloat16 [65536, 256], P(('loop', 'grp'))
All inputs are finite; a program needn't handle non-finite values.
Results may differ from a plain program's by a relative error of at most 0.0046.
Values may be sent and summed in bfloat16 or wider, within the bound.
No kernel may reach another device: no remote copies, remote signals or barrier semaphores. Data moves between devices by JAX's collectives and lax.ppermute only.
A program may use at most 128 MiB of HBM per device.

v0:
```python
import jax
import jax.numpy as jnp
from jax import lax
from jax.sharding import PartitionSpec as P


def on_device(adjacency_tiles, row_block, column_block, features, weight, out_bias):
    tile_size = adjacency_tiles.shape[1]
    feat_width = features.shape[1]
    loop_count = lax.axis_size("loop")
    section_rows = lax.all_gather(features, "grp", axis=0, tiled=True)
    section_blocks = section_rows.reshape(-1, tile_size, feat_width)
    picked = jnp.take(section_blocks, column_block, axis=0)
    products = jnp.einsum(
        "tij,tjf->tif", adjacency_tiles, picked, preferred_element_type=jnp.float32
    )
    partial_value = jax.ops.segment_sum(products, row_block, num_segments=loop_count)
    summed = lax.psum_scatter(partial_value, "loop", scatter_dimension=0, tiled=True)
    aggregate = summed.reshape(tile_size, feat_width).astype(jnp.bfloat16)
    mixed = jnp.dot(aggregate, weight, preferred_element_type=jnp.float32) + out_bias
    return jax.nn.relu(mixed).astype(jnp.bfloat16)


def solution(mesh):
    in_specs = (
        P(("loop", "grp"), None, None),
        P(("loop", "grp")),
        P(("loop", "grp")),
        P(("loop", "grp"), None),
        P(),
        P(),
    )
    out_specs = P(("loop", "grp"), None)
    return jax.shard_map(
        on_device, mesh=mesh, in_specs=in_specs, out_specs=out_specs, check_vma=False
    )
```

profile of v0, /device:TPU:24, one launch (start us, length us, event | category | flops | bytes accessed | tf_op | source)
XLA Modules:
  0.0 333.1 jit_solution(5589250887956877626)
XLA Ops:
  6.5 0.0 copy-start
  6.5 0.0 all-gather.2.cloned.1.call-start
  6.5 0.7 all-gather.2.cloned.1.call-update
  7.3 0.0 reduce-scatter.2.cloned.1.call-start
  7.3 0.7 compare_select_fusion
  8.0 0.7 compare_and_fusion
  8.6 83.3 %all-gather.2.cloned.1.call-done = bf16[2048,256]{1,0:T(8,128)(2,1)} async-done(((bf16[128,256]{1,0:T(8,128)(2,1)}), bf16[2048,256]{1,0:T(8,128)(2,1)}) %all-gather.2.cloned.1.call-update) | async-done | bytes 1048592 | tf_op jit(solution)/shard_map/all_gather | solution.py:11
  91.9 7.8 %gather_fusion = bf16[128,128,256]{2,1,0:T(8,128)(2,1)} fusion(bf16[16,128,256]{2,1,0:T(8,128)(2,1)} %bitcast.8, s32[1024]{0:T(1024)S(1)} %pad_clamp_fusion), kind=kCustom, calls=%fused_computation | custom fusion | bytes 16777728 | tf_op jit(solution)/shard_map/jit(_take)/gather | solution.py:13
  99.7 13.1 %convolution_bitcast_fusion = f32[128,128,256]{1,2,0:T(8,128)} fusion(bf16[128,128,128]{2,1,0:T(8,128)(2,1)} %param.6, bf16[128,128,256]{2,1,0:T(8,128)(2,1)} %gather_fusion, pred[128]{0:T(512)(128)(4,1)S(1)} %compare_and_fusion), kind=kOutput, calls=%fused_computation.2 | convolution fusion | flops 1077936128 | bytes 29360256 | tf_op jit(solution)/shard_map/tij,tjf->tif/dot_general | solution.py:14
  112.8 0.0 copy-start.2
  112.8 17.5 %copy.9 = f32[128,128,256]{2,1,0:T(8,128)} copy(f32[128,128,256]{1,2,0:T(8,128)} %convolution_bitcast_fusion) | data formatting | bytes 33554432 | tf_op jit(solution)/shard_map/tij,tjf->tif/dot_general | solution.py:14
  130.3 2.4 broadcast_in_dim.19
  132.7 0.0 copy-done.2
  132.7 0.0 copy-start.1
  132.7 37.6 %scatter_fusion = f32[32,128,256]{2,1,0:T(8,128)} fusion(f32[32,128,256]{2,1,0:T(8,128)} %broadcast_in_dim.19, s32[128]{0:T(128)S(1)} %copy-done.2, f32[128,128,256]{2,1,0:T(8,128)} %copy.9), kind=kCustom, calls=%fused_computation.1 | custom fusion | flops 4194304 | bytes 50332160 | tf_op jit(solution)/shard_map/scatter-add | solution.py:17
  170.3 0.0 reduce-scatter.2.cloned.1.call-update
  170.3 154.2 %reduce-scatter.2.cloned.1.call-done = f32[1,128,256]{2,1,0:T(8,128)} async-done(((f32[32,128,256]{2,1,0:T(8,128)}), f32[1,128,256]{2,1,0:T(8,128)}) %reduce-scatter.2.cloned.1.call-update) | async-done | bytes 131088 | tf_op jit(solution)/shard_map/reduce_scatter | solution.py:18
  324.5 0.0 copy-done
  324.5 0.0 copy-done.1
  324.5 1.7 fusion.4
  (1 shorter events, 0.0 us)
Async XLA Ops:
  6.5 318.0 %copy-start = (bf16[256,256]{1,0:T(8,128)(2,1)S(1)}, bf16[256,256]{1,0:T(8,128)(2,1)}, u32[]{:S(2)}) copy-start(bf16[256,256]{1,0:T(8,128)(2,1)} %param.10) | copy-start | bytes 393220
  6.5 85.4 %all-gather.2.cloned.1.call-start = ((), (), s32[]{:S(2)}) async-start(), calls=%async_computation.1 | async-start | bytes 1114112 | tf_op jit(solution)/shard_map/all_gather | solution.py:11
  7.3 317.3 %reduce-scatter.2.cloned.1.call-start = ((), (), s32[]{:S(2)}) async-start(), calls=%async_computation.2 | async-start | bytes 4325376 | tf_op jit(solution)/shard_map/reduce_scatter | solution.py:18
  112.8 19.9 %copy-start.2 = (s32[128]{0:T(128)S(1)}, s32[128]{0:T(128)}, u32[]{:S(2)}) copy-start(s32[128]{0:T(128)} %param.7) | copy-start | bytes 1540
  132.7 191.8 %copy-start.1 = (f32[256]{0:T(256)S(1)}, f32[256]{0:T(256)}, u32[]{:S(2)}) copy-start(f32[256]{0:T(256)} %param.11) | copy-start | bytes 3076
Sparse Core Ops, SparseCore 0:
  10.3 81.5 all-gather.1
  170.5 154.0 reduce-scatter.1
where the time goes:
time: 334 us; the launch traced here: 333 us
  waiting for transfers between devices  238 us (71%)
  other arithmetic  38.9 us (12%)
  local copies, waits for them, and re-layouts  27.7 us (8%)
  matrix products  14.8 us (4%)
  between operations  13.4 us (4%)
    reduce_scatter x1, waiting for transfers between devices, on_device(): lax.psum_scatter(partial_value, 'loop', scatter_dimension=0, tiled=True)  154 us
    all_gather x1, waiting for transfers between devices, on_device(): section_rows = lax.all_gather(features, 'grp', axis=0, tiled=True)  83.3 us
    scatter-add x1, other arithmetic, on_device(): jax.ops.segment_sum(products, row_block, num_segments=loop_count)  37.6 us
    dot_general x1, local copies, waits for them, and re-layouts, on_device(): jnp.einsum('tij,tjf->tif', adjacency_tiles, picked, preferred_element_typ...  17.5 us
    dot_general x1, matrix products, on_device(): jnp.einsum('tij,tjf->tif', adjacency_tiles, picked, preferred_element_typ...  13.1 us
    gather x1, local copies, waits for them, and re-layouts, on_device(): picked = jnp.take(section_blocks, column_block, axis=0)  7.78 us
  transfers between devices with their start and end apart: 2, of which 2 were waited for; matrix products, arithmetic and copies ran while one was open for 0% of the time, Pallas kernels for 0%

commit v1 on v0

--- a/solution.py
+++ b/solution.py
@@ -8,7 +8,9 @@
     tile_size = adjacency_tiles.shape[1]
     feat_width = features.shape[1]
     loop_count = lax.axis_size("loop")
-    section_rows = lax.all_gather(features, "grp", axis=0, tiled=True)
+    section_rows = jnp.concatenate(
+        lax.all_to_all(jnp.stack([features] * lax.axis_size("grp")), "grp", 0, 0), axis=0
+    )
     section_blocks = section_rows.reshape(-1, tile_size, feat_width)
     picked = jnp.take(section_blocks, column_block, axis=0)
     products = jnp.einsum(

time: 334 us -> 320 us (0.958)
  waiting for transfers between devices: 238 us -> 205 us
  starting transfers between devices: 0.04 us -> 18 us
    all_gather x1 -> x0, waiting for transfers between devices: 83.3 us -> none  [on_device(): section_rows = lax.all_gather(features, 'grp', axis=0, tiled=True)]
    all_to_all x0 -> x1, waiting for transfers between devices: none -> 49.4 us  [on_device(): lax.all_to_all(jnp.stack([features] * lax.axis_size('grp')), 'grp', 0, 0)]
    all_to_all x0 -> x1, starting transfers between devices: none -> 18 us  [on_device(): lax.all_to_all(jnp.stack([features] * lax.axis_size('grp')), 'grp', 0, 0)]
where the time goes in v1:
time: 320 us; the launch traced here: 319 us
  waiting for transfers between devices  205 us (64%)
  other arithmetic  39 us (12%)
  local copies, waits for them, and re-layouts  28.4 us (9%)
  starting transfers between devices  18 us (6%)
  matrix products  14.9 us (5%)
  between operations  13.4 us (4%)
    reduce_scatter x1, waiting for transfers between devices, on_device(): lax.psum_scatter(partial_value, 'loop', scatter_dimension=0, tiled=True)  156 us
    all_to_all x1, waiting for transfers between devices, on_device(): lax.all_to_all(jnp.stack([features] * lax.axis_size('grp')), 'grp', 0, 0)  49.4 us
    scatter-add x1, other arithmetic, on_device(): jax.ops.segment_sum(products, row_block, num_segments=loop_count)  37.7 us
    all_to_all x1, starting transfers between devices, on_device(): lax.all_to_all(jnp.stack([features] * lax.axis_size('grp')), 'grp', 0, 0)  18 us
    dot_general x1, local copies, waits for them, and re-layouts, on_device(): jnp.einsum('tij,tjf->tif', adjacency_tiles, picked, preferred_element_typ...  17.5 us
    dot_general x1, matrix products, on_device(): jnp.einsum('tij,tjf->tif', adjacency_tiles, picked, preferred_element_typ...  13.2 us
    gather x1, local copies, waits for them, and re-layouts, on_device(): picked = jnp.take(section_blocks, column_block, axis=0)  6.56 us
  transfers between devices with their start and end apart: 2, of which 2 were waited for; matrix products, arithmetic and copies ran while one was open for 0% of the time, Pallas kernels for 0%

profile of v1, /device:TPU:24, one launch (start us, length us, event | category | flops | bytes accessed | tf_op | source)
XLA Modules:
  0.0 319.3 jit_solution(15235057991997245929)
XLA Ops:
  6.5 0.0 copy-start
  6.5 1.9 stack.2
  8.5 18.0 %all-to-all-start = ((bf16[16,128,256]{2,1,0:T(8,128)(2,1)}), bf16[16,128,256]{2,1,0:T(8,128)(2,1)S(1)}, u32[]{:S(2)}, u32[]{:S(2)}) async-start(bf16[16,128,256]{2,1,0:T(8,128)(2,1)} %stack.2), calls=%async_computation | async-start | bytes 2097152 | tf_op jit(solution)/shard_map/all_to_all | solution.py:12
  26.4 0.0 reduce-scatter.2.cloned.1.call-start
  26.5 0.7 compare_select_fusion
  27.2 0.7 compare_and_fusion
  27.8 49.4 %all-to-all-done = bf16[16,128,256]{2,1,0:T(8,128)(2,1)S(1)} async-done(((bf16[16,128,256]{2,1,0:T(8,128)(2,1)}), bf16[16,128,256]{2,1,0:T(8,128)(2,1)S(1)}, u32[]{:S(2)}, u32[]{:S(2)}) %all-to-all-start) | async-done | bytes 1048608 | tf_op jit(solution)/shard_map/all_to_all | solution.py:12
  77.2 6.6 %gather_fusion = bf16[128,128,256]{2,1,0:T(8,128)(2,1)} fusion(bf16[16,128,256]{2,1,0:T(8,128)(2,1)S(1)} %all-to-all-done, s32[1024]{0:T(1024)S(1)} %pad_clamp_fusion), kind=kCustom, calls=%fused_computation | custom fusion | bytes 16777728 | tf_op jit(solution)/shard_map/jit(_take)/gather | solution.py:15
  83.7 13.2 %convolution_bitcast_fusion = f32[128,128,256]{1,2,0:T(8,128)} fusion(bf16[128,128,128]{2,1,0:T(8,128)(2,1)} %param.6, bf16[128,128,256]{2,1,0:T(8,128)(2,1)} %gather_fusion, pred[128]{0:T(512)(128)(4,1)S(1)} %compare_and_fusion), kind=kOutput, calls=%fused_computation.2 | convolution fusion | flops 1077936128 | bytes 29360256 | tf_op jit(solution)/shard_map/tij,tjf->tif/dot_general | solution.py:16
  97.0 0.0 copy-start.2
  97.0 17.5 %copy.9 = f32[128,128,256]{2,1,0:T(8,128)} copy(f32[128,128,256]{1,2,0:T(8,128)} %convolution_bitcast_fusion) | data formatting | bytes 33554432 | tf_op jit(solution)/shard_map/tij,tjf->tif/dot_general | solution.py:16
  114.4 2.4 broadcast_in_dim.19
  116.9 0.0 copy-done.2
  116.9 0.0 copy-start.1
  116.9 37.7 %scatter_fusion = f32[32,128,256]{2,1,0:T(8,128)} fusion(f32[32,128,256]{2,1,0:T(8,128)} %broadcast_in_dim.19, s32[128]{0:T(128)S(1)} %copy-done.2, f32[128,128,256]{2,1,0:T(8,128)} %copy.9), kind=kCustom, calls=%fused_computation.1 | custom fusion | flops 4194304 | bytes 50332160 | tf_op jit(solution)/shard_map/scatter-add | solution.py:19
  154.6 0.0 reduce-scatter.2.cloned.1.call-update
  154.6 156.1 %reduce-scatter.2.cloned.1.call-done = f32[1,128,256]{2,1,0:T(8,128)} async-done(((f32[32,128,256]{2,1,0:T(8,128)}), f32[1,128,256]{2,1,0:T(8,128)}) %reduce-scatter.2.cloned.1.call-update) | async-done | bytes 131088 | tf_op jit(solution)/shard_map/reduce_scatter | solution.py:20
  310.7 0.0 copy-done
  310.7 0.0 copy-done.1
  310.7 1.7 fusion.4
  (1 shorter events, 0.0 us)
Async XLA Ops:
  6.5 304.2 %copy-start = (bf16[256,256]{1,0:T(8,128)(2,1)S(1)}, bf16[256,256]{1,0:T(8,128)(2,1)}, u32[]{:S(2)}) copy-start(bf16[256,256]{1,0:T(8,128)(2,1)} %param.10) | copy-start | bytes 393220
  8.5 68.7 %all-to-all-start = ((bf16[16,128,256]{2,1,0:T(8,128)(2,1)}), bf16[16,128,256]{2,1,0:T(8,128)(2,1)S(1)}, u32[]{:S(2)}, u32[]{:S(2)}) async-start(bf16[16,128,256]{2,1,0:T(8,128)(2,1)} %stack.2), calls=%async_computation | async-start | bytes 2097152 | tf_op jit(solution)/shard_map/all_to_all | solution.py:12
  26.4 284.3 %reduce-scatter.2.cloned.1.call-start = ((), (), s32[]{:S(2)}) async-start(), calls=%async_computation.2 | async-start | bytes 4325376 | tf_op jit(solution)/shard_map/reduce_scatter | solution.py:20
  97.0 19.9 %copy-start.2 = (s32[128]{0:T(128)S(1)}, s32[128]{0:T(128)}, u32[]{:S(2)}) copy-start(s32[128]{0:T(128)} %param.7) | copy-start | bytes 1540
  116.9 193.8 %copy-start.1 = (f32[256]{0:T(256)S(1)}, f32[256]{0:T(256)}, u32[]{:S(2)}) copy-start(f32[256]{0:T(256)} %param.11) | copy-start | bytes 3076
Sparse Core Ops, SparseCore 0:
  154.7 155.9 reduce-scatter.1
